TPU v7x, 512 devices: a whole 4x8x8 slice. The times are simulated.
512 devices in a mesh: row: 64 (over z, x, core), col: 8 (over y).
Axes of the slice: x: 4, y: 8, z: 8, core: 2. Of those that a mesh axis runs over, the one named last changes fastest.
Arguments:
- amplitudes: bfloat16 [512, 256, 256], P('col', 'row'), may hold values from -6 to 6
- integrals: bfloat16 [256, 48, 256, 256], P('row', 'col'), may hold values from -0.03125 to 0.03125
- screen: int32 [256, 48], P('row', 'col'), may hold values from -1 to 7, as said below
- owner_map: int32 [8, 8], P('col'), may hold values from 0 to 7, each once within a row
Outputs:
- ladder: float32 [512, 64, 256], P('row', 'col')
Inputs may be any that keep to these rules, and one draw needn't show every extreme that they name: `screen`: in each row and column group the 6 slots first name distinct result tiles of that group, then hold -1; at least 2 are live, and some group of some row has all 6 live.
All inputs are finite; a program needn't handle non-finite values.
Results may differ from a plain program's by a relative error of at most 0.0003.
Values may be sent and summed in bfloat16 or wider, within the bound.
A program may use at most 64 MiB of HBM per device.

v0:
```python
import jax
import jax.numpy as jnp
from jax import lax
from jax.sharding import PartitionSpec as P


def body(amplitudes, integrals, screen, owner_map):
    gathered = lax.all_gather(amplitudes, "col", axis=0, tiled=True)
    group_tiles = owner_map.shape[1]
    live_slot = screen >= 0
    labels = jnp.arange(group_tiles, dtype=jnp.int32)
    matches = screen[:, :, None] == labels[None, None, :]
    stored = jnp.sum(jnp.where(matches, owner_map[0][None, None, :], 0), axis=2)
    selector = ((stored[:, :, None] == labels[None, None, :]) & live_slot[:, :, None]).astype(
        jnp.bfloat16
    )
    placed = jnp.einsum(
        "kla,klwv->kawv", selector, integrals, preferred_element_type=jnp.float32
    ).astype(jnp.bfloat16)
    return lax.psum_scatter(
        jnp.einsum("pkw,kawv->pav", gathered, placed, preferred_element_type=jnp.float32),
        "row",
        scatter_dimension=0,
        tiled=True,
    )


def solution(mesh):
    return jax.shard_map(
        body,
        mesh=mesh,
        in_specs=(
            P("col", "row", None),
            P("row", "col", None, None),
            P("row", "col"),
            P("col", None),
        ),
        out_specs=P("row", "col", None),
        check_vma=False,
    )
```

profile of v0, /device:TPU:8, one launch (start us, length us, event | category | flops | bytes accessed | tf_op | source)
XLA Modules:
  0.0 226.7 jit_solution(1776103147567017797)
XLA Ops:
  6.5 0.0 copy-start
  6.5 0.0 all-gather.2.cloned.1.call-start
  6.5 1.7 copy.12
  8.2 0.0 all-gather.2.cloned.1.call-update
  8.3 0.0 reduce-scatter.2.cloned.1.call-start
  8.3 0.8 copy.9
  9.1 0.9 select_reduce_fusion
  10.0 0.1 copy.10
  10.1 0.7 broadcast_compare_fusion
  10.8 0.0 copy-done
  10.8 3.9 %fusion.4 = bf16[4,8,256,256]{3,1,2,0:T(8,128)(2,1)} fusion(bf16[4,6,256,256]{3,2,1,0:T(8,128)(2,1)S(1)} %copy-done, s32[4,6]{1,0:T(4,128)S(1)} %copy.10, pred[4,6]{1,0:T(4,128)(4,1)S(1)} %broadcast_compare_fusion), kind=kOutput, calls=%fused_computation.4 | convolution fusion | flops 27263360 | bytes 7340152 | tf_op jit(solution)/shard_map/kla,klwv->kawv/dot_general | solution.py:17
  14.7 39.9 %all-gather.2.cloned.1.call-done = bf16[512,4,256]{2,0,1:T(8,128)(2,1)} async-done(((bf16[64,4,256]{2,0,1:T(8,128)(2,1)}), bf16[512,4,256]{2,0,1:T(8,128)(2,1)}) %all-gather.2.cloned.1.call-update) | async-done | bytes 1048592 | tf_op jit(solution)/shard_map/all_gather | solution.py:8
  54.6 7.1 %fusion.7 = f32[512,8,256]{0,2,1:T(8,128)} fusion(bf16[4,8,256,256]{3,1,2,0:T(8,128)(2,1)} %fusion.4, bf16[512,4,256]{2,0,1:T(8,128)(2,1)} %all-gather.2.cloned.1.call-done), kind=kOutput, calls=%fused_computation.5 | convolution fusion | flops 2147483648 | bytes 9437184 | tf_op jit(solution)/shard_map/pkw,kawv->pav/dot_general | solution.py:21
  61.7 5.4 %copy.14 = f32[512,8,256]{2,1,0:T(8,128)} copy(f32[512,8,256]{0,2,1:T(8,128)} %fusion.7) | data formatting | bytes 8388608 | tf_op jit(solution)/shard_map/pkw,kawv->pav/dot_general | solution.py:21
  67.2 0.0 reduce-scatter.2.cloned.1.call-update
  67.2 152.7 %reduce-scatter.2.cloned.1.call-done = f32[8,8,256]{2,1,0:T(8,128)} async-done(((f32[512,8,256]{2,1,0:T(8,128)}), f32[8,8,256]{2,1,0:T(8,128)}) %reduce-scatter.2.cloned.1.call-update) | async-done | bytes 65552 | tf_op jit(solution)/shard_map/reduce_scatter | solution.py:20
Async XLA Ops:
  6.5 4.2 %copy-start = (bf16[4,6,256,256]{3,2,1,0:T(8,128)(2,1)S(1)}, bf16[4,6,256,256]{3,2,1,0:T(8,128)(2,1)}, u32[]{:S(2)}) copy-start(bf16[4,6,256,256]{3,2,1,0:T(8,128)(2,1)} %param.5) | copy-start | bytes 9437188
  6.5 48.1 %all-gather.2.cloned.1.call-start = ((), (), s32[]{:S(2)}) async-start(), calls=%async_computation.1 | async-start | bytes 1179648 | tf_op jit(solution)/shard_map/all_gather | solution.py:8
  8.3 211.6 %reduce-scatter.2.cloned.1.call-start = ((), (), s32[]{:S(2)}) async-start(), calls=%async_computation.2 | async-start | bytes 4259840 | tf_op jit(solution)/shard_map/reduce_scatter | solution.py:20
Sparse Core Ops, SparseCore 0:
  9.4 45.1 all-gather.1
  67.3 152.4 reduce-scatter.1
where the time goes:
time: 227 us
  waiting for transfers between devices  193 us (85%)
  between operations  13.4 us (6%)
  matrix products  11.1 us (5%)
  local copies, waits for them, and re-layouts  8.01 us (4%)
    reduce_scatter x1, waiting for transfers between devices, body(): lax.psum_scatter(jnp.einsum('pkw,kawv->pav', gathered, placed, preferred_...  153 us
    all_gather x1, waiting for transfers between devices, body(): gathered = lax.all_gather(amplitudes, 'col', axis=0, tiled=True)  39.9 us
    dot_general x1, matrix products, body(): jnp.einsum('pkw,kawv->pav', gathered, placed, preferred_element_type=jnp....  7.13 us
    dot_general x1, local copies, waits for them, and re-layouts, body(): jnp.einsum('pkw,kawv->pav', gathered, placed, preferred_element_type=jnp....  5.44 us
  transfers between devices with their start and end apart: 2, of which 2 were waited for; matrix products, arithmetic and copies ran while one was open for 3% of the time, Pallas kernels for 0%

commit v1 on v0

--- a/solution.py
+++ b/solution.py
@@ -1,11 +1,23 @@
+import functools
 import jax
 import jax.numpy as jnp
 from jax import lax
 from jax.sharding import PartitionSpec as P
 
 
+def report_islands(tile_in, mesh_name):
+    opened = jnp.concatenate(
+        jax.lax.all_to_all(jnp.stack(jax.lax.axis_size(mesh_name) * [tile_in]), mesh_name, 0, 0),
+        axis=0,
+    )
+    return opened
+
+
+solve_ways_here = functools.partial(report_islands, mesh_name="col")
+
+
 def body(amplitudes, integrals, screen, owner_map):
-    gathered = lax.all_gather(amplitudes, "col", axis=0, tiled=True)
+    gathered = solve_ways_here(amplitudes)
     group_tiles = owner_map.shape[1]
     live_slot = screen >= 0
     labels = jnp.arange(group_tiles, dtype=jnp.int32)

time: 227 us -> 218 us (0.960)
  waiting for transfers between devices: 193 us -> 173 us
  starting transfers between devices: 0.04 us -> 9.92 us
    all_gather x1 -> x0, waiting for transfers between devices: 39.9 us -> none  [body(): gathered = lax.all_gather(amplitudes, 'col', axis=0, tiled=True)]
    all_to_all x0 -> x1, waiting for transfers between devices: none -> 18.6 us  [report_islands(): jax.lax.all_to_all(jnp.stack(jax.lax.axis_size(mesh_name) * [tile_in]), m...]
    all_to_all x0 -> x1, starting transfers between devices: none -> 9.91 us  [report_islands(): jax.lax.all_to_all(jnp.stack(jax.lax.axis_size(mesh_name) * [tile_in]), m...]
where the time goes in v1:
time: 218 us
  waiting for transfers between devices  173 us (79%)
  between operations  13.4 us (6%)
  matrix products  10.8 us (5%)
  starting transfers between devices  9.92 us (5%)
  local copies, waits for them, and re-layouts  9.83 us (5%)
    reduce_scatter x1, waiting for transfers between devices, body(): lax.psum_scatter(jnp.einsum('pkw,kawv->pav', gathered, placed, preferred_...  154 us
    all_to_all x1, waiting for transfers between devices, report_islands(): jax.lax.all_to_all(jnp.stack(jax.lax.axis_size(mesh_name) * [tile_in]), m...  18.6 us
    all_to_all x1, starting transfers between devices, report_islands(): jax.lax.all_to_all(jnp.stack(jax.lax.axis_size(mesh_name) * [tile_in]), m...  9.91 us
    dot_general x1, matrix products, body(): jnp.einsum('pkw,kawv->pav', gathered, placed, preferred_element_type=jnp....  6.85 us
    dot_general x1, local copies, waits for them, and re-layouts, body(): jnp.einsum('pkw,kawv->pav', gathered, placed, preferred_element_type=jnp....  5.44 us
  transfers between devices with their start and end apart: 2, of which 2 were waited for; matrix products, arithmetic and copies ran while one was open for 3% of the time, Pallas kernels for 0%

profile of v1, /device:TPU:8, one launch (start us, length us, event | category | flops | bytes accessed | tf_op | source)
XLA Modules:
  0.0 218.0 jit_solution(3774469857860281567)
XLA Ops:
  6.5 0.0 copy-start
  6.5 1.1 copy.13
  7.6 1.1 stack.2
  8.7 9.9 %all-to-all-start = ((bf16[8,64,4,256]{3,1,2,0:T(8,128)(2,1)}), bf16[8,64,4,256]{3,1,2,0:T(8,128)(2,1)}, u32[]{:S(2)}, u32[]{:S(2)}) async-start(bf16[8,64,4,256]{3,1,2,0:T(8,128)(2,1)} %stack.2), calls=%async_computation | async-start | bytes 2097152 | tf_op jit(solution)/shard_map/all_to_all | solution.py:10
  18.7 0.0 reduce-scatter.2.cloned.1.call-start
  18.7 0.8 copy.10
  19.4 0.9 select_reduce_fusion
  20.3 0.1 copy.11
  20.4 0.7 broadcast_compare_fusion
  21.1 0.0 copy-done
  21.1 3.9 %fusion.4 = bf16[4,8,256,256]{3,1,2,0:T(8,128)(2,1)} fusion(bf16[4,6,256,256]{3,2,1,0:T(8,128)(2,1)S(1)} %copy-done, s32[4,6]{1,0:T(4,128)S(1)} %copy.11, pred[4,6]{1,0:T(4,128)(4,1)S(1)} %broadcast_compare_fusion), kind=kOutput, calls=%fused_computation.4 | convolution fusion | flops 27263360 | bytes 7340152 | tf_op jit(solution)/shard_map/kla,klwv->kawv/dot_general | solution.py:29
  25.0 18.6 %all-to-all-done = bf16[8,64,4,256]{3,1,2,0:T(8,128)(2,1)} async-done(((bf16[8,64,4,256]{3,1,2,0:T(8,128)(2,1)}), bf16[8,64,4,256]{3,1,2,0:T(8,128)(2,1)}, u32[]{:S(2)}, u32[]{:S(2)}) %all-to-all-start) | async-done | bytes 1048608 | tf_op jit(solution)/shard_map/all_to_all | solution.py:10
  43.7 1.3 copy.14
  45.0 6.9 %fusion.7 = f32[512,8,256]{0,2,1:T(8,128)} fusion(bf16[512,4,256,1]{2,0,1,3:T(8,128)(2,1)S(1)} %bitcast.15, bf16[4,8,256,256]{3,1,2,0:T(8,128)(2,1)} %fusion.4), kind=kOutput, calls=%fused_computation.5 | convolution fusion | flops 2147483648 | bytes 9437184 | tf_op jit(solution)/shard_map/pkw,kawv->pav/dot_general | solution.py:33
  51.9 5.4 %copy.16 = f32[512,8,256]{2,1,0:T(8,128)} copy(f32[512,8,256]{0,2,1:T(8,128)} %fusion.7) | data formatting | bytes 8388608 | tf_op jit(solution)/shard_map/pkw,kawv->pav/dot_general | solution.py:33
  57.3 0.0 reduce-scatter.2.cloned.1.call-update
  57.3 153.9 %reduce-scatter.2.cloned.1.call-done = f32[8,8,256]{2,1,0:T(8,128)} async-done(((f32[512,8,256]{2,1,0:T(8,128)}), f32[8,8,256]{2,1,0:T(8,128)}) %reduce-scatter.2.cloned.1.call-update) | async-done | bytes 65552 | tf_op jit(solution)/shard_map/reduce_scatter | solution.py:32
Async XLA Ops:
  6.5 14.6 %copy-start = (bf16[4,6,256,256]{3,2,1,0:T(8,128)(2,1)S(1)}, bf16[4,6,256,256]{3,2,1,0:T(8,128)(2,1)}, u32[]{:S(2)}) copy-start(bf16[4,6,256,256]{3,2,1,0:T(8,128)(2,1)} %param.5) | copy-start | bytes 9437188
  8.7 34.9 %all-to-all-start = ((bf16[8,64,4,256]{3,1,2,0:T(8,128)(2,1)}), bf16[8,64,4,256]{3,1,2,0:T(8,128)(2,1)}, u32[]{:S(2)}, u32[]{:S(2)}) async-start(bf16[8,64,4,256]{3,1,2,0:T(8,128)(2,1)} %stack.2), calls=%async_computation | async-start | bytes 2097152 | tf_op jit(solution)/shard_map/all_to_all | solution.py:10
  18.7 192.5 %reduce-scatter.2.cloned.1.call-start = ((), (), s32[]{:S(2)}) async-start(), calls=%async_computation.2 | async-start | bytes 4259840 | tf_op jit(solution)/shard_map/reduce_scatter | solution.py:32
Sparse Core Ops, SparseCore 0:
  57.4 153.7 reduce-scatter.1
